TPU v7x, 512 devices: a whole 4x4x16 slice. The times are simulated.
512 devices in a mesh: space: 128 (over z, y, x_lo), shot: 4 (over x_hi, core).
Axes of the slice: x: 4 (x_hi: 2, x_lo: 2; x = x_hi * 2 + x_lo), y: 4, z: 16, core: 2. Of those that a mesh axis runs over, the one named last changes fastest.
Arguments:
- velocity: float32 [1024, 192, 128], P('space'), may hold values from 1.5 to 4.5
- wave_now: float32 [4, 1024, 192, 128], P('shot', 'space'), may hold values from -6 to 6
- wave_prev: float32 [4, 1024, 192, 128], P('shot', 'space'), may hold values from -6 to 6
- adjoint_now: float32 [4, 1024, 192, 128], P('shot', 'space'), may hold values from -6 to 6
- adjoint_prev: float32 [4, 1024, 192, 128], P('shot', 'space'), may hold values from -6 to 6
- source_cells: int32 [4, 128], P('shot'), may hold values from 0 to 25165823, as said below
- wavelet: float32 [4, 10, 128], P('shot'), may hold values from -24 to 24
- receiver_cells: int32 [65536], P('space'), may hold values from 0 to 196607, as said below
- receiver_counts: int32 [128], P('space'), may hold values from 128 to 512, as said below
- observed: float32 [4, 10, 65536], P('shot', None, 'space'), may hold values from -24 to 24
Outputs:
- gradient: float32 [1024, 192, 128], P('space', 'shot')
Inputs may be any that keep to these rules, and one draw needn't show every extreme that they name: `source_cells`: flat indices into the whole grid (first dimension slowest); the 128 cells of one shot group are distinct. `receiver_cells`: flat indices within one device's block of 8 x 192 x 128 cells (first dimension slowest); the 512 cells of one block are distinct. `receiver_counts`: the live slots of a block come first.
All inputs are finite; a program needn't handle non-finite values.
Results may differ from a plain program's by a relative error of at most 0.00002.
Values sent between devices are 32-bit elements; how exact they have to be, the bound alone decides.
No kernel may reach another device: no remote copies, remote signals or barrier semaphores. Data moves between devices by JAX's collectives and lax.ppermute only.
A program may use at most 64 MiB of HBM per device.

v0:
```python
import jax
import jax.numpy as jnp
from jax import lax
from jax.sharding import PartitionSpec as P

TAPS = (-205.0 / 72.0, 8.0 / 5.0, -1.0 / 5.0, 8.0 / 315.0, -1.0 / 560.0)
COURANT = 0.09


def with_halo(block, sides, width):
    for axis, dim in sides:
        count = lax.axis_size(axis)
        forward = [(i, i + 1) for i in range(count - 1)]
        backward = [(target, source) for source, target in forward]
        low = lax.ppermute(
            lax.slice_in_dim(block, block.shape[dim] - width, None, axis=dim), axis, forward
        )
        high = lax.ppermute(lax.slice_in_dim(block, 0, width, axis=dim), axis, backward)
        block = jnp.concatenate([low, block, high], axis=dim)
    return block


def laplace(widened):
    length_x = widened.shape[0] - 8
    extent_y = widened.shape[1]
    extent_z = widened.shape[2]
    padded = jnp.pad(widened, ((0, 0), (4, 4), (4, 4)))
    centre = widened[4 : 4 + length_x]
    result = 3.0 * TAPS[0] * centre
    for distance in range(1, 5):
        beside_all = (
            padded[4 + distance : 4 + distance + length_x, 4 : 4 + extent_y, 4 : 4 + extent_z]
            + padded[4 - distance : 4 - distance + length_x, 4 : 4 + extent_y, 4 : 4 + extent_z]
        )
        beside_all = (
            beside_all
            + padded[4 : 4 + length_x, 4 + distance : 4 + distance + extent_y, 4 : 4 + extent_z]
            + padded[4 : 4 + length_x, 4 - distance : 4 - distance + extent_y, 4 : 4 + extent_z]
        )
        beside_all = (
            beside_all
            + padded[4 : 4 + length_x, 4 : 4 + extent_y, 4 + distance : 4 + distance + extent_z]
            + padded[4 : 4 + length_x, 4 : 4 + extent_y, 4 - distance : 4 - distance + extent_z]
        )
        result = result + TAPS[distance] * beside_all
    return result


def edge_layers(field):
    return with_halo(field, (("space", 0),), 4)


def add_at(field, target, amounts):
    size_all = field.size
    inside = (target >= 0) & (target < size_all)
    flat_field = (
        field.reshape(-1).at[jnp.where(inside, target, 0)].add(jnp.where(inside, amounts, 0.0))
    )
    return flat_field.reshape(field.shape)


def per_device(
    velocity,
    wave_now,
    wave_prev,
    adjoint_now,
    adjoint_prev,
    source_cells,
    wavelet,
    receiver_cells,
    receiver_counts,
    observed,
):
    extent_x, extent_y, extent_z = velocity.shape
    plane_cells = extent_y * extent_z
    courant_sq = (COURANT * velocity) ** 2
    position = lax.axis_index("space")
    local_sources = source_cells[0] - position * (extent_x * plane_cells)
    pulses = wavelet[0]

    def forward(carried, source_pulse):
        current, former = carried
        latest = 2.0 * current - former + courant_sq * laplace(edge_layers(current))
        latest = add_at(latest, local_sources, source_pulse)
        acceleration = latest - 2.0 * current + former
        return ((latest, current), (acceleration, latest.reshape(-1)[receiver_cells]))

    _, (accelerations, traces) = lax.scan(forward, (wave_now[0], wave_prev[0]), pulses)
    live_slots = (jnp.arange(receiver_cells.shape[0], dtype=jnp.int32) < receiver_counts[0]).astype(
        jnp.float32
    )
    misfit = (traces - observed[0]) * live_slots

    def backward(carried, inputs):
        following, furthest, imaging = carried
        acceleration, residual = inputs
        earlier = 2.0 * following - furthest + courant_sq * laplace(edge_layers(following))
        earlier = earlier.reshape(-1).at[receiver_cells].add(residual).reshape(velocity.shape)
        return ((earlier, following, imaging + earlier * acceleration), None)

    empty_field = jnp.zeros_like(velocity)
    (_, _, imaging), _ = lax.scan(
        backward,
        (adjoint_now[0], adjoint_prev[0], empty_field),
        (accelerations, misfit),
        reverse=True,
    )
    band_rows = extent_y // lax.axis_size("shot")
    offset = lax.axis_index("shot") * band_rows
    factor = lax.dynamic_slice_in_dim(-2.0 / velocity**3, offset, band_rows, 1)
    summed = lax.psum(imaging, "shot")
    own_band = lax.dynamic_slice_in_dim(summed, offset, band_rows, 1)
    return factor * own_band


def solution(mesh):
    in_specs = (
        P("space", None, None),
        P("shot", "space", None, None),
        P("shot", "space", None, None),
        P("shot", "space", None, None),
        P("shot", "space", None, None),
        P("shot", None),
        P("shot", None, None),
        P("space"),
        P("space"),
        P("shot", None, "space"),
    )
    out_specs = P("space", "shot", None)
    return jax.shard_map(
        per_device, mesh=mesh, in_specs=in_specs, out_specs=out_specs, check_vma=False
    )
```

profile of v0, /device:TPU:1, one launch (start us, length us, event | category | flops | bytes accessed | tf_op | source)
XLA Modules:
  0.0 773.0 jit_solution(16620281286347901368)
XLA Ops:
  12.2 333.3 %while.37 = (s32[]{:T(128)}, f32[8,192,128]{2,1,0:T(8,128)S(1)}, f32[8,192,128]{2,1,0:T(8,128)}, f32[10,8,192,128]{3,2,1,0:T(8,128)}, f32[10,512]{1,0:T(8,128)},...) while((s32[]{:T(128)}, f32[8,192,128]{2,1,0:T(8,128)S(1)}, ...), condition=%wide.region_2.3_spmd, body=%wide.region_0.2_spmd.sunk | while | flops 13609986 | bytes 43449096 | solution.py:88
  13.0 4.0 collective-permute-start.1
  22.2 13.2 %collective-permute-done = f32[4,192,128]{2,1,0:T(8,128)S(1)} collective-permute-done((f32[4,192,128]{2,1,0:T(8,128)S(1)}, f32[4,192,128]{2,1,0:T(8,128)S(1)}, u32[]{:S(2)}, u32[]{:S(2)}) %collective-permute-start) | collective-permute-done | bytes 393248 | tf_op jit(solution)/shard_map/while/body/eval_jaxpr/ppermute | solution.py:18
  36.4 3.3 fusion.41
  56.1 4.0 collective-permute-done.1
  60.3 10.1 %collective-permute-done = f32[4,192,128]{2,1,0:T(8,128)S(1)} collective-permute-done((f32[4,192,128]{2,1,0:T(8,128)S(1)}, f32[4,192,128]{2,1,0:T(8,128)S(1)}, u32[]{:S(2)}, u32[]{:S(2)}) %collective-permute-start) | collective-permute-done | bytes 393248 | tf_op jit(solution)/shard_map/while/body/eval_jaxpr/ppermute | solution.py:18
  71.4 3.3 fusion.41
  94.5 9.8 %collective-permute-done = f32[4,192,128]{2,1,0:T(8,128)S(1)} collective-permute-done((f32[4,192,128]{2,1,0:T(8,128)S(1)}, f32[4,192,128]{2,1,0:T(8,128)S(1)}, u32[]{:S(2)}, u32[]{:S(2)}) %collective-permute-start) | collective-permute-done | bytes 393248 | tf_op jit(solution)/shard_map/while/body/eval_jaxpr/ppermute | solution.py:18
  105.3 3.3 fusion.41
  127.4 9.7 %collective-permute-done = f32[4,192,128]{2,1,0:T(8,128)S(1)} collective-permute-done((f32[4,192,128]{2,1,0:T(8,128)S(1)}, f32[4,192,128]{2,1,0:T(8,128)S(1)}, u32[]{:S(2)}, u32[]{:S(2)}) %collective-permute-start) | collective-permute-done | bytes 393248 | tf_op jit(solution)/shard_map/while/body/eval_jaxpr/ppermute | solution.py:18
  138.1 3.3 fusion.41
  159.2 8.4 %collective-permute-done = f32[4,192,128]{2,1,0:T(8,128)S(1)} collective-permute-done((f32[4,192,128]{2,1,0:T(8,128)S(1)}, f32[4,192,128]{2,1,0:T(8,128)S(1)}, u32[]{:S(2)}, u32[]{:S(2)}) %collective-permute-start) | collective-permute-done | bytes 393248 | tf_op jit(solution)/shard_map/while/body/eval_jaxpr/ppermute | solution.py:18
  190.1 8.0 %collective-permute-done = f32[4,192,128]{2,1,0:T(8,128)S(1)} collective-permute-done((f32[4,192,128]{2,1,0:T(8,128)S(1)}, f32[4,192,128]{2,1,0:T(8,128)S(1)}, u32[]{:S(2)}, u32[]{:S(2)}) %collective-permute-start) | collective-permute-done | bytes 393248 | tf_op jit(solution)/shard_map/while/body/eval_jaxpr/ppermute | solution.py:18
  219.2 5.9 collective-permute-done
  245.8 4.1 collective-permute-done.1
  250.1 10.8 %collective-permute-done = f32[4,192,128]{2,1,0:T(8,128)S(1)} collective-permute-done((f32[4,192,128]{2,1,0:T(8,128)S(1)}, f32[4,192,128]{2,1,0:T(8,128)S(1)}, u32[]{:S(2)}, u32[]{:S(2)}) %collective-permute-start) | collective-permute-done | bytes 393248 | tf_op jit(solution)/shard_map/while/body/eval_jaxpr/ppermute | solution.py:18
  261.8 3.3 fusion.41
  275.3 5.2 collective-permute-start.1
  285.8 11.1 %collective-permute-done = f32[4,192,128]{2,1,0:T(8,128)S(1)} collective-permute-done((f32[4,192,128]{2,1,0:T(8,128)S(1)}, f32[4,192,128]{2,1,0:T(8,128)S(1)}, u32[]{:S(2)}, u32[]{:S(2)}) %collective-permute-start) | collective-permute-done | bytes 393248 | tf_op jit(solution)/shard_map/while/body/eval_jaxpr/ppermute | solution.py:18
  311.3 5.2 collective-permute-start.1
  321.8 10.1 %collective-permute-done = f32[4,192,128]{2,1,0:T(8,128)S(1)} collective-permute-done((f32[4,192,128]{2,1,0:T(8,128)S(1)}, f32[4,192,128]{2,1,0:T(8,128)S(1)}, u32[]{:S(2)}, u32[]{:S(2)}) %collective-permute-start) | collective-permute-done | bytes 393248 | tf_op jit(solution)/shard_map/while/body/eval_jaxpr/ppermute | solution.py:18
  346.9 325.5 %while.38 = (s32[]{:T(128)}, f32[8,192,128]{2,1,0:T(8,128)S(1)}, f32[8,192,128]{2,1,0:T(8,128)}, f32[8,192,128]{2,1,0:T(8,128)}, f32[8,192,128]{2,1,0:T(8,128)S(...) while((s32[]{:T(128)}, f32[8,192,128]{2,1,0:T(8,128)S(1)}, ...), condition=%wide.region_5.6_spmd.clone, body=%wide.region_3.5_spmd.clone.sunk | while | flops 13607940 | bytes 49729836 | solution.py:102
  347.0 4.9 collective-permute-start.3
  357.0 6.4 collective-permute-done.2
  368.6 3.7 scatter_fusion.1
  375.0 5.3 collective-permute-start.3
  382.4 12.6 %collective-permute-done.3 = f32[4,192,128]{2,1,0:T(8,128)S(1)} collective-permute-done((f32[4,192,128]{2,1,0:T(8,128)S(1)}, f32[4,192,128]{2,1,0:T(8,128)S(1)}, u32[]{:S(2)}, u32[]{:S(2)}) %collective-permute-start.3) | collective-permute-done | bytes 393248 | tf_op jit(solution)/shard_map/while/body/eval_jaxpr/ppermute | solution.py:15
  395.2 5.2 collective-permute-done.2
  401.3 3.3 fusion.44
  405.6 3.7 scatter_fusion.1
  412.1 5.3 collective-permute-start.3
  419.4 3.3 collective-permute-done.3
  422.9 10.5 %collective-permute-done.2 = f32[4,192,128]{2,1,0:T(8,128)S(1)} collective-permute-done((f32[4,192,128]{2,1,0:T(8,128)S(1)}, f32[4,192,128]{2,1,0:T(8,128)S(1)}, u32[]{:S(2)}, u32[]{:S(2)}) %collective-permute-start.2) | collective-permute-done | bytes 393248 | tf_op jit(solution)/shard_map/while/body/eval_jaxpr/ppermute | solution.py:18
  434.3 3.3 fusion.44
  438.6 3.7 scatter_fusion.1
  445.0 5.2 collective-permute-start.3
  452.3 5.2 collective-permute-done.3
  457.7 7.9 %collective-permute-done.2 = f32[4,192,128]{2,1,0:T(8,128)S(1)} collective-permute-done((f32[4,192,128]{2,1,0:T(8,128)S(1)}, f32[4,192,128]{2,1,0:T(8,128)S(1)}, u32[]{:S(2)}, u32[]{:S(2)}) %collective-permute-start.2) | collective-permute-done | bytes 393248 | tf_op jit(solution)/shard_map/while/body/eval_jaxpr/ppermute | solution.py:18
  470.8 3.7 scatter_fusion.1
  477.3 5.3 collective-permute-start.3
  484.7 5.9 collective-permute-done.3
  490.7 3.4 collective-permute-done.2
  499.3 3.7 scatter_fusion.1
  505.8 4.7 collective-permute-start.3
  512.5 12.5 %collective-permute-done.3 = f32[4,192,128]{2,1,0:T(8,128)S(1)} collective-permute-done((f32[4,192,128]{2,1,0:T(8,128)S(1)}, f32[4,192,128]{2,1,0:T(8,128)S(1)}, u32[]{:S(2)}, u32[]{:S(2)}) %collective-permute-start.3) | collective-permute-done | bytes 393248 | tf_op jit(solution)/shard_map/while/body/eval_jaxpr/ppermute | solution.py:15
  525.3 5.4 collective-permute-done.2
  535.9 3.7 scatter_fusion.1
  542.4 5.0 collective-permute-start.3
  549.4 3.4 collective-permute-done.3
  553.0 10.7 %collective-permute-done.2 = f32[4,192,128]{2,1,0:T(8,128)S(1)} collective-permute-done((f32[4,192,128]{2,1,0:T(8,128)S(1)}, f32[4,192,128]{2,1,0:T(8,128)S(1)}, u32[]{:S(2)}, u32[]{:S(2)}) %collective-permute-start.2) | collective-permute-done | bytes 393248 | tf_op jit(solution)/shard_map/while/body/eval_jaxpr/ppermute | solution.py:18
  568.9 3.7 scatter_fusion.1
  575.4 5.0 collective-permute-start.3
  582.4 5.3 collective-permute-done.3
  587.8 7.9 %collective-permute-done.2 = f32[4,192,128]{2,1,0:T(8,128)S(1)} collective-permute-done((f32[4,192,128]{2,1,0:T(8,128)S(1)}, f32[4,192,128]{2,1,0:T(8,128)S(1)}, u32[]{:S(2)}, u32[]{:S(2)}) %collective-permute-start.2) | collective-permute-done | bytes 393248 | tf_op jit(solution)/shard_map/while/body/eval_jaxpr/ppermute | solution.py:18
  601.0 3.7 scatter_fusion.1
  607.4 5.3 collective-permute-start.3
  614.8 5.9 collective-permute-done.3
  620.8 3.4 collective-permute-done.2
  629.5 3.7 scatter_fusion.1
  635.9 4.7 collective-permute-start.3
  642.6 12.6 %collective-permute-done.3 = f32[4,192,128]{2,1,0:T(8,128)S(1)} collective-permute-done((f32[4,192,128]{2,1,0:T(8,128)S(1)}, f32[4,192,128]{2,1,0:T(8,128)S(1)}, u32[]{:S(2)}, u32[]{:S(2)}) %collective-permute-start.3) | collective-permute-done | bytes 393248 | tf_op jit(solution)/shard_map/while/body/eval_jaxpr/ppermute | solution.py:15
  655.4 5.4 collective-permute-done.2
  666.0 3.7 scatter_fusion.1
  672.5 92.0 %all-reduce.4.cloned.1.call-done = f32[8,192,128]{2,1,0:T(8,128)} async-done(((f32[8,192,128]{2,1,0:T(8,128)}), f32[8,192,128]{2,1,0:T(8,128)}) %all-reduce.4.cloned.1.call-update) | async-done | bytes 786448 | tf_op jit(solution)/shard_map/psum | solution.py:111
  (426 shorter events, 300.9 us)
Async XLA Ops:
  6.5 757.9 %all-reduce.4.cloned.1.call-start = ((), (), s32[]{:S(2)}) async-start(), calls=%async_computation | async-start | bytes 1572864 | tf_op jit(solution)/shard_map/psum | solution.py:111
  6.5 5.1 copy-start.11
  6.5 5.7 copy-start
  6.6 5.7 copy-start.8
  12.2 334.7 %copy-start.1 = (f32[1,8,192,128]{3,2,1,0:T(8,128)S(1)}, f32[1,8,192,128]{3,2,1,0:T(8,128)}, u32[]{:S(2)}) copy-start(f32[1,8,192,128]{3,2,1,0:T(8,128)} %param.17) | copy-start | bytes 2359300
  13.0 9.0 %collective-permute-start.1 = (f32[4,192,128]{2,1,0:T(8,128)}, f32[4,192,128]{2,1,0:T(8,128)S(1)}, u32[]{:S(2)}, u32[]{:S(2)}) collective-permute-start(f32[4,192,128]{2,1,0:T(8,128)} %get-tuple-element.457), channel_id=1, source_target_pairs={{0,4},{4,8},{8,12},{12,16},{16,20},{20,24},{24,28},{28,32},{32,36}... | collective-permute-start | bytes 1179656 | tf_op jit(solution)/shard_map/while/body/eval_jaxpr/ppermute | solution.py:15
  17.0 18.4 %collective-permute-start = (f32[4,192,128]{2,1,0:T(8,128)S(1)}, f32[4,192,128]{2,1,0:T(8,128)S(1)}, u32[]{:S(2)}, u32[]{:S(2)}) collective-permute-start(f32[4,192,128]{2,1,0:T(8,128)S(1)} %get-tuple-element.456), channel_id=1, source_target_pairs={{4,0},{8,4},{12,8},{16,12},{20,16},{24,20},{28,24},{32,28},{36,32}... | collective-permute-start | bytes 1179656 | tf_op jit(solution)/shard_map/while/body/eval_jaxpr/ppermute | solution.py:18
  22.2 14.2 %copy-start.2 = (f32[8,192,128]{2,1,0:T(8,128)S(1)}, f32[8,192,128]{2,1,0:T(8,128)}, u32[]{:S(2)}) copy-start(f32[8,192,128]{2,1,0:T(8,128)} %get-tuple-element.485) | copy-start | bytes 2359300 | tf_op jit(solution)/shard_map/while
  49.9 10.3 %collective-permute-start.1 = (f32[4,192,128]{2,1,0:T(8,128)}, f32[4,192,128]{2,1,0:T(8,128)S(1)}, u32[]{:S(2)}, u32[]{:S(2)}) collective-permute-start(f32[4,192,128]{2,1,0:T(8,128)} %get-tuple-element.457), channel_id=1, source_target_pairs={{0,4},{4,8},{8,12},{12,16},{16,20},{20,24},{24,28},{28,32},{32,36}... | collective-permute-start | bytes 1179656 | tf_op jit(solution)/shard_map/while/body/eval_jaxpr/ppermute | solution.py:15
  53.0 17.5 %collective-permute-start = (f32[4,192,128]{2,1,0:T(8,128)S(1)}, f32[4,192,128]{2,1,0:T(8,128)S(1)}, u32[]{:S(2)}, u32[]{:S(2)}) collective-permute-start(f32[4,192,128]{2,1,0:T(8,128)S(1)} %get-tuple-element.456), channel_id=1, source_target_pairs={{4,0},{8,4},{12,8},{16,12},{20,16},{24,20},{28,24},{32,28},{36,32}... | collective-permute-start | bytes 1179656 | tf_op jit(solution)/shard_map/while/body/eval_jaxpr/ppermute | solution.py:18
  60.3 11.1 %copy-start.2 = (f32[8,192,128]{2,1,0:T(8,128)S(1)}, f32[8,192,128]{2,1,0:T(8,128)}, u32[]{:S(2)}) copy-start(f32[8,192,128]{2,1,0:T(8,128)} %get-tuple-element.485) | copy-start | bytes 2359300 | tf_op jit(solution)/shard_map/while
  84.9 9.3 %collective-permute-start.1 = (f32[4,192,128]{2,1,0:T(8,128)}, f32[4,192,128]{2,1,0:T(8,128)S(1)}, u32[]{:S(2)}, u32[]{:S(2)}) collective-permute-start(f32[4,192,128]{2,1,0:T(8,128)} %get-tuple-element.457), channel_id=1, source_target_pairs={{0,4},{4,8},{8,12},{12,16},{16,20},{20,24},{24,28},{28,32},{32,36}... | collective-permute-start | bytes 1179656 | tf_op jit(solution)/shard_map/while/body/eval_jaxpr/ppermute | solution.py:15
  88.1 16.2 %collective-permute-start = (f32[4,192,128]{2,1,0:T(8,128)S(1)}, f32[4,192,128]{2,1,0:T(8,128)S(1)}, u32[]{:S(2)}, u32[]{:S(2)}) collective-permute-start(f32[4,192,128]{2,1,0:T(8,128)S(1)} %get-tuple-element.456), channel_id=1, source_target_pairs={{4,0},{8,4},{12,8},{16,12},{20,16},{24,20},{28,24},{32,28},{36,32}... | collective-permute-start | bytes 1179656 | tf_op jit(solution)/shard_map/while/body/eval_jaxpr/ppermute | solution.py:18
  94.5 10.8 %copy-start.2 = (f32[8,192,128]{2,1,0:T(8,128)S(1)}, f32[8,192,128]{2,1,0:T(8,128)}, u32[]{:S(2)}) copy-start(f32[8,192,128]{2,1,0:T(8,128)} %get-tuple-element.485) | copy-start | bytes 2359300 | tf_op jit(solution)/shard_map/while
  118.8 8.4 %collective-permute-start.1 = (f32[4,192,128]{2,1,0:T(8,128)}, f32[4,192,128]{2,1,0:T(8,128)S(1)}, u32[]{:S(2)}, u32[]{:S(2)}) collective-permute-start(f32[4,192,128]{2,1,0:T(8,128)} %get-tuple-element.457), channel_id=1, source_target_pairs={{0,4},{4,8},{8,12},{12,16},{16,20},{20,24},{24,28},{28,32},{32,36}... | collective-permute-start | bytes 1179656 | tf_op jit(solution)/shard_map/while/body/eval_jaxpr/ppermute | solution.py:15
  121.9 15.2 %collective-permute-start = (f32[4,192,128]{2,1,0:T(8,128)S(1)}, f32[4,192,128]{2,1,0:T(8,128)S(1)}, u32[]{:S(2)}, u32[]{:S(2)}) collective-permute-start(f32[4,192,128]{2,1,0:T(8,128)S(1)} %get-tuple-element.456), channel_id=1, source_target_pairs={{4,0},{8,4},{12,8},{16,12},{20,16},{24,20},{28,24},{32,28},{36,32}... | collective-permute-start | bytes 1179656 | tf_op jit(solution)/shard_map/while/body/eval_jaxpr/ppermute | solution.py:18
  127.4 10.7 %copy-start.2 = (f32[8,192,128]{2,1,0:T(8,128)S(1)}, f32[8,192,128]{2,1,0:T(8,128)}, u32[]{:S(2)}) copy-start(f32[8,192,128]{2,1,0:T(8,128)} %get-tuple-element.485) | copy-start | bytes 2359300 | tf_op jit(solution)/shard_map/while
  151.5 7.5 collective-permute-start.1
  154.0 13.6 %collective-permute-start = (f32[4,192,128]{2,1,0:T(8,128)S(1)}, f32[4,192,128]{2,1,0:T(8,128)S(1)}, u32[]{:S(2)}, u32[]{:S(2)}) collective-permute-start(f32[4,192,128]{2,1,0:T(8,128)S(1)} %get-tuple-element.456), channel_id=1, source_target_pairs={{4,0},{8,4},{12,8},{16,12},{20,16},{24,20},{28,24},{32,28},{36,32}... | collective-permute-start | bytes 1179656 | tf_op jit(solution)/shard_map/while/body/eval_jaxpr/ppermute | solution.py:18
  159.2 9.4 %copy-start.2 = (f32[8,192,128]{2,1,0:T(8,128)S(1)}, f32[8,192,128]{2,1,0:T(8,128)}, u32[]{:S(2)}) copy-start(f32[8,192,128]{2,1,0:T(8,128)} %get-tuple-element.485) | copy-start | bytes 2359300 | tf_op jit(solution)/shard_map/while
  182.1 7.8 %collective-permute-start.1 = (f32[4,192,128]{2,1,0:T(8,128)}, f32[4,192,128]{2,1,0:T(8,128)S(1)}, u32[]{:S(2)}, u32[]{:S(2)}) collective-permute-start(f32[4,192,128]{2,1,0:T(8,128)} %get-tuple-element.457), channel_id=1, source_target_pairs={{0,4},{4,8},{8,12},{12,16},{16,20},{20,24},{24,28},{28,32},{32,36}... | collective-permute-start | bytes 1179656 | tf_op jit(solution)/shard_map/while/body/eval_jaxpr/ppermute | solution.py:15
  184.9 13.2 %collective-permute-start = (f32[4,192,128]{2,1,0:T(8,128)S(1)}, f32[4,192,128]{2,1,0:T(8,128)S(1)}, u32[]{:S(2)}, u32[]{:S(2)}) collective-permute-start(f32[4,192,128]{2,1,0:T(8,128)S(1)} %get-tuple-element.456), channel_id=1, source_target_pairs={{4,0},{8,4},{12,8},{16,12},{20,16},{24,20},{28,24},{32,28},{36,32}... | collective-permute-start | bytes 1179656 | tf_op jit(solution)/shard_map/while/body/eval_jaxpr/ppermute | solution.py:18
  190.0 9.0 %copy-start.2 = (f32[8,192,128]{2,1,0:T(8,128)S(1)}, f32[8,192,128]{2,1,0:T(8,128)}, u32[]{:S(2)}) copy-start(f32[8,192,128]{2,1,0:T(8,128)} %get-tuple-element.485) | copy-start | bytes 2359300 | tf_op jit(solution)/shard_map/while
  212.5 6.5 collective-permute-start.1
  214.0 11.1 %collective-permute-start = (f32[4,192,128]{2,1,0:T(8,128)S(1)}, f32[4,192,128]{2,1,0:T(8,128)S(1)}, u32[]{:S(2)}, u32[]{:S(2)}) collective-permute-start(f32[4,192,128]{2,1,0:T(8,128)S(1)} %get-tuple-element.456), channel_id=1, source_target_pairs={{4,0},{8,4},{12,8},{16,12},{20,16},{24,20},{28,24},{32,28},{36,32}... | collective-permute-start | bytes 1179656 | tf_op jit(solution)/shard_map/while/body/eval_jaxpr/ppermute | solution.py:18
  219.2 6.9 copy-start.2
  239.6 10.3 %collective-permute-start.1 = (f32[4,192,128]{2,1,0:T(8,128)}, f32[4,192,128]{2,1,0:T(8,128)S(1)}, u32[]{:S(2)}, u32[]{:S(2)}) collective-permute-start(f32[4,192,128]{2,1,0:T(8,128)} %get-tuple-element.457), channel_id=1, source_target_pairs={{0,4},{4,8},{8,12},{12,16},{16,20},{20,24},{24,28},{28,32},{32,36}... | collective-permute-start | bytes 1179656 | tf_op jit(solution)/shard_map/while/body/eval_jaxpr/ppermute | solution.py:15
  242.6 18.3 %collective-permute-start = (f32[4,192,128]{2,1,0:T(8,128)S(1)}, f32[4,192,128]{2,1,0:T(8,128)S(1)}, u32[]{:S(2)}, u32[]{:S(2)}) collective-permute-start(f32[4,192,128]{2,1,0:T(8,128)S(1)} %get-tuple-element.456), channel_id=1, source_target_pairs={{4,0},{8,4},{12,8},{16,12},{20,16},{24,20},{28,24},{32,28},{36,32}... | collective-permute-start | bytes 1179656 | tf_op jit(solution)/shard_map/while/body/eval_jaxpr/ppermute | solution.py:18
  250.0 11.8 %copy-start.2 = (f32[8,192,128]{2,1,0:T(8,128)S(1)}, f32[8,192,128]{2,1,0:T(8,128)}, u32[]{:S(2)}) copy-start(f32[8,192,128]{2,1,0:T(8,128)} %get-tuple-element.485) | copy-start | bytes 2359300 | tf_op jit(solution)/shard_map/while
  275.3 10.2 %collective-permute-start.1 = (f32[4,192,128]{2,1,0:T(8,128)}, f32[4,192,128]{2,1,0:T(8,128)S(1)}, u32[]{:S(2)}, u32[]{:S(2)}) collective-permute-start(f32[4,192,128]{2,1,0:T(8,128)} %get-tuple-element.457), channel_id=1, source_target_pairs={{0,4},{4,8},{8,12},{12,16},{16,20},{20,24},{24,28},{28,32},{32,36}... | collective-permute-start | bytes 1179656 | tf_op jit(solution)/shard_map/while/body/eval_jaxpr/ppermute | solution.py:15
  280.6 16.3 %collective-permute-start = (f32[4,192,128]{2,1,0:T(8,128)S(1)}, f32[4,192,128]{2,1,0:T(8,128)S(1)}, u32[]{:S(2)}, u32[]{:S(2)}) collective-permute-start(f32[4,192,128]{2,1,0:T(8,128)S(1)} %get-tuple-element.456), channel_id=1, source_target_pairs={{4,0},{8,4},{12,8},{16,12},{20,16},{24,20},{28,24},{32,28},{36,32}... | collective-permute-start | bytes 1179656 | tf_op jit(solution)/shard_map/while/body/eval_jaxpr/ppermute | solution.py:18
  285.8 12.0 %copy-start.2 = (f32[8,192,128]{2,1,0:T(8,128)S(1)}, f32[8,192,128]{2,1,0:T(8,128)}, u32[]{:S(2)}) copy-start(f32[8,192,128]{2,1,0:T(8,128)} %get-tuple-element.485) | copy-start | bytes 2359300 | tf_op jit(solution)/shard_map/while
  311.3 10.2 %collective-permute-start.1 = (f32[4,192,128]{2,1,0:T(8,128)}, f32[4,192,128]{2,1,0:T(8,128)S(1)}, u32[]{:S(2)}, u32[]{:S(2)}) collective-permute-start(f32[4,192,128]{2,1,0:T(8,128)} %get-tuple-element.457), channel_id=1, source_target_pairs={{0,4},{4,8},{8,12},{12,16},{16,20},{20,24},{24,28},{28,32},{32,36}... | collective-permute-start | bytes 1179656 | tf_op jit(solution)/shard_map/while/body/eval_jaxpr/ppermute | solution.py:15
  316.6 15.3 %collective-permute-start = (f32[4,192,128]{2,1,0:T(8,128)S(1)}, f32[4,192,128]{2,1,0:T(8,128)S(1)}, u32[]{:S(2)}, u32[]{:S(2)}) collective-permute-start(f32[4,192,128]{2,1,0:T(8,128)S(1)} %get-tuple-element.456), channel_id=1, source_target_pairs={{4,0},{8,4},{12,8},{16,12},{20,16},{24,20},{28,24},{32,28},{36,32}... | collective-permute-start | bytes 1179656 | tf_op jit(solution)/shard_map/while/body/eval_jaxpr/ppermute | solution.py:18
  321.8 11.1 %copy-start.2 = (f32[8,192,128]{2,1,0:T(8,128)S(1)}, f32[8,192,128]{2,1,0:T(8,128)}, u32[]{:S(2)}) copy-start(f32[8,192,128]{2,1,0:T(8,128)} %get-tuple-element.485) | copy-start | bytes 2359300 | tf_op jit(solution)/shard_map/while
  347.0 9.8 %collective-permute-start.3 = (f32[4,192,128]{2,1,0:T(8,128)S(1)}, f32[4,192,128]{2,1,0:T(8,128)S(1)}, u32[]{:S(2)}, u32[]{:S(2)}) collective-permute-start(f32[4,192,128]{2,1,0:T(8,128)S(1)} %get-tuple-element.469), channel_id=1, source_target_pairs={{0,4},{4,8},{8,12},{12,16},{16,20},{20,24},{24,28},{28,32},{32,36}... | collective-permute-start | bytes 1179656 | tf_op jit(solution)/shard_map/while/body/eval_jaxpr/ppermute | solution.py:15
  351.9 11.4 %collective-permute-start.2 = (f32[4,192,128]{2,1,0:T(8,128)S(1)}, f32[4,192,128]{2,1,0:T(8,128)S(1)}, u32[]{:S(2)}, u32[]{:S(2)}) collective-permute-start(f32[4,192,128]{2,1,0:T(8,128)S(1)} %get-tuple-element.468), channel_id=1, source_target_pairs={{4,0},{8,4},{12,8},{16,12},{20,16},{24,20},{28,24},{32,28},{36,32}... | collective-permute-start | bytes 1179656 | tf_op jit(solution)/shard_map/while/body/eval_jaxpr/ppermute | solution.py:18
  357.0 7.3 copy-start.3
  375.0 20.0 %collective-permute-start.3 = (f32[4,192,128]{2,1,0:T(8,128)S(1)}, f32[4,192,128]{2,1,0:T(8,128)S(1)}, u32[]{:S(2)}, u32[]{:S(2)}) collective-permute-start(f32[4,192,128]{2,1,0:T(8,128)S(1)} %get-tuple-element.469), channel_id=1, source_target_pairs={{0,4},{4,8},{8,12},{12,16},{16,20},{20,24},{24,28},{28,32},{32,36}... | collective-permute-start | bytes 1179656 | tf_op jit(solution)/shard_map/while/body/eval_jaxpr/ppermute | solution.py:15
  380.4 20.0 %collective-permute-start.2 = (f32[4,192,128]{2,1,0:T(8,128)S(1)}, f32[4,192,128]{2,1,0:T(8,128)S(1)}, u32[]{:S(2)}, u32[]{:S(2)}) collective-permute-start(f32[4,192,128]{2,1,0:T(8,128)S(1)} %get-tuple-element.468), channel_id=1, source_target_pairs={{4,0},{8,4},{12,8},{16,12},{20,16},{24,20},{28,24},{32,28},{36,32}... | collective-permute-start | bytes 1179656 | tf_op jit(solution)/shard_map/while/body/eval_jaxpr/ppermute | solution.py:18
  395.2 6.1 copy-start.3
  412.1 10.6 %collective-permute-start.3 = (f32[4,192,128]{2,1,0:T(8,128)S(1)}, f32[4,192,128]{2,1,0:T(8,128)S(1)}, u32[]{:S(2)}, u32[]{:S(2)}) collective-permute-start(f32[4,192,128]{2,1,0:T(8,128)S(1)} %get-tuple-element.469), channel_id=1, source_target_pairs={{0,4},{4,8},{8,12},{12,16},{16,20},{20,24},{24,28},{28,32},{32,36}... | collective-permute-start | bytes 1179656 | tf_op jit(solution)/shard_map/while/body/eval_jaxpr/ppermute | solution.py:15
  417.3 16.0 %collective-permute-start.2 = (f32[4,192,128]{2,1,0:T(8,128)S(1)}, f32[4,192,128]{2,1,0:T(8,128)S(1)}, u32[]{:S(2)}, u32[]{:S(2)}) collective-permute-start(f32[4,192,128]{2,1,0:T(8,128)S(1)} %get-tuple-element.468), channel_id=1, source_target_pairs={{4,0},{8,4},{12,8},{16,12},{20,16},{24,20},{28,24},{32,28},{36,32}... | collective-permute-start | bytes 1179656 | tf_op jit(solution)/shard_map/while/body/eval_jaxpr/ppermute | solution.py:18
  422.9 11.5 %copy-start.3 = (f32[8,192,128]{2,1,0:T(8,128)S(1)}, f32[8,192,128]{2,1,0:T(8,128)}, u32[]{:S(2)}) copy-start(f32[8,192,128]{2,1,0:T(8,128)} %get-tuple-element.518) | copy-start | bytes 2359300 | tf_op jit(solution)/shard_map/while
  445.0 12.5 %collective-permute-start.3 = (f32[4,192,128]{2,1,0:T(8,128)S(1)}, f32[4,192,128]{2,1,0:T(8,128)S(1)}, u32[]{:S(2)}, u32[]{:S(2)}) collective-permute-start(f32[4,192,128]{2,1,0:T(8,128)S(1)} %get-tuple-element.469), channel_id=1, source_target_pairs={{0,4},{4,8},{8,12},{12,16},{16,20},{20,24},{24,28},{28,32},{32,36}... | collective-permute-start | bytes 1179656 | tf_op jit(solution)/shard_map/while/body/eval_jaxpr/ppermute | solution.py:15
  450.3 15.4 %collective-permute-start.2 = (f32[4,192,128]{2,1,0:T(8,128)S(1)}, f32[4,192,128]{2,1,0:T(8,128)S(1)}, u32[]{:S(2)}, u32[]{:S(2)}) collective-permute-start(f32[4,192,128]{2,1,0:T(8,128)S(1)} %get-tuple-element.468), channel_id=1, source_target_pairs={{4,0},{8,4},{12,8},{16,12},{20,16},{24,20},{28,24},{32,28},{36,32}... | collective-permute-start | bytes 1179656 | tf_op jit(solution)/shard_map/while/body/eval_jaxpr/ppermute | solution.py:18
  457.7 8.9 %copy-start.3 = (f32[8,192,128]{2,1,0:T(8,128)S(1)}, f32[8,192,128]{2,1,0:T(8,128)}, u32[]{:S(2)}) copy-start(f32[8,192,128]{2,1,0:T(8,128)} %get-tuple-element.518) | copy-start | bytes 2359300 | tf_op jit(solution)/shard_map/while
  477.3 13.2 %collective-permute-start.3 = (f32[4,192,128]{2,1,0:T(8,128)S(1)}, f32[4,192,128]{2,1,0:T(8,128)S(1)}, u32[]{:S(2)}, u32[]{:S(2)}) collective-permute-start(f32[4,192,128]{2,1,0:T(8,128)S(1)} %get-tuple-element.469), channel_id=1, source_target_pairs={{0,4},{4,8},{8,12},{12,16},{16,20},{20,24},{24,28},{28,32},{32,36}... | collective-permute-start | bytes 1179656 | tf_op jit(solution)/shard_map/while/body/eval_jaxpr/ppermute | solution.py:15
  482.6 11.5 %collective-permute-start.2 = (f32[4,192,128]{2,1,0:T(8,128)S(1)}, f32[4,192,128]{2,1,0:T(8,128)S(1)}, u32[]{:S(2)}, u32[]{:S(2)}) collective-permute-start(f32[4,192,128]{2,1,0:T(8,128)S(1)} %get-tuple-element.468), channel_id=1, source_target_pairs={{4,0},{8,4},{12,8},{16,12},{20,16},{24,20},{28,24},{32,28},{36,32}... | collective-permute-start | bytes 1179656 | tf_op jit(solution)/shard_map/while/body/eval_jaxpr/ppermute | solution.py:18
  490.7 4.4 copy-start.3
  505.8 19.3 %collective-permute-start.3 = (f32[4,192,128]{2,1,0:T(8,128)S(1)}, f32[4,192,128]{2,1,0:T(8,128)S(1)}, u32[]{:S(2)}, u32[]{:S(2)}) collective-permute-start(f32[4,192,128]{2,1,0:T(8,128)S(1)} %get-tuple-element.469), channel_id=1, source_target_pairs={{0,4},{4,8},{8,12},{12,16},{16,20},{20,24},{24,28},{28,32},{32,36}... | collective-permute-start | bytes 1179656 | tf_op jit(solution)/shard_map/while/body/eval_jaxpr/ppermute | solution.py:15
  510.5 20.2 %collective-permute-start.2 = (f32[4,192,128]{2,1,0:T(8,128)S(1)}, f32[4,192,128]{2,1,0:T(8,128)S(1)}, u32[]{:S(2)}, u32[]{:S(2)}) collective-permute-start(f32[4,192,128]{2,1,0:T(8,128)S(1)} %get-tuple-element.468), channel_id=1, source_target_pairs={{4,0},{8,4},{12,8},{16,12},{20,16},{24,20},{28,24},{32,28},{36,32}... | collective-permute-start | bytes 1179656 | tf_op jit(solution)/shard_map/while/body/eval_jaxpr/ppermute | solution.py:18
  525.3 6.4 copy-start.3
  542.4 10.4 %collective-permute-start.3 = (f32[4,192,128]{2,1,0:T(8,128)S(1)}, f32[4,192,128]{2,1,0:T(8,128)S(1)}, u32[]{:S(2)}, u32[]{:S(2)}) collective-permute-start(f32[4,192,128]{2,1,0:T(8,128)S(1)} %get-tuple-element.469), channel_id=1, source_target_pairs={{0,4},{4,8},{8,12},{12,16},{16,20},{20,24},{24,28},{28,32},{32,36}... | collective-permute-start | bytes 1179656 | tf_op jit(solution)/shard_map/while/body/eval_jaxpr/ppermute | solution.py:15
  547.3 16.4 %collective-permute-start.2 = (f32[4,192,128]{2,1,0:T(8,128)S(1)}, f32[4,192,128]{2,1,0:T(8,128)S(1)}, u32[]{:S(2)}, u32[]{:S(2)}) collective-permute-start(f32[4,192,128]{2,1,0:T(8,128)S(1)} %get-tuple-element.468), channel_id=1, source_target_pairs={{4,0},{8,4},{12,8},{16,12},{20,16},{24,20},{28,24},{32,28},{36,32}... | collective-permute-start | bytes 1179656 | tf_op jit(solution)/shard_map/while/body/eval_jaxpr/ppermute | solution.py:18
  553.0 11.7 %copy-start.3 = (f32[8,192,128]{2,1,0:T(8,128)S(1)}, f32[8,192,128]{2,1,0:T(8,128)}, u32[]{:S(2)}) copy-start(f32[8,192,128]{2,1,0:T(8,128)} %get-tuple-element.518) | copy-start | bytes 2359300 | tf_op jit(solution)/shard_map/while
  575.4 12.3 %collective-permute-start.3 = (f32[4,192,128]{2,1,0:T(8,128)S(1)}, f32[4,192,128]{2,1,0:T(8,128)S(1)}, u32[]{:S(2)}, u32[]{:S(2)}) collective-permute-start(f32[4,192,128]{2,1,0:T(8,128)S(1)} %get-tuple-element.469), channel_id=1, source_target_pairs={{0,4},{4,8},{8,12},{12,16},{16,20},{20,24},{24,28},{28,32},{32,36}... | collective-permute-start | bytes 1179656 | tf_op jit(solution)/shard_map/while/body/eval_jaxpr/ppermute | solution.py:15
  580.3 15.4 %collective-permute-start.2 = (f32[4,192,128]{2,1,0:T(8,128)S(1)}, f32[4,192,128]{2,1,0:T(8,128)S(1)}, u32[]{:S(2)}, u32[]{:S(2)}) collective-permute-start(f32[4,192,128]{2,1,0:T(8,128)S(1)} %get-tuple-element.468), channel_id=1, source_target_pairs={{4,0},{8,4},{12,8},{16,12},{20,16},{24,20},{28,24},{32,28},{36,32}... | collective-permute-start | bytes 1179656 | tf_op jit(solution)/shard_map/while/body/eval_jaxpr/ppermute | solution.py:18
  587.8 8.9 %copy-start.3 = (f32[8,192,128]{2,1,0:T(8,128)S(1)}, f32[8,192,128]{2,1,0:T(8,128)}, u32[]{:S(2)}) copy-start(f32[8,192,128]{2,1,0:T(8,128)} %get-tuple-element.518) | copy-start | bytes 2359300 | tf_op jit(solution)/shard_map/while
  607.4 13.2 %collective-permute-start.3 = (f32[4,192,128]{2,1,0:T(8,128)S(1)}, f32[4,192,128]{2,1,0:T(8,128)S(1)}, u32[]{:S(2)}, u32[]{:S(2)}) collective-permute-start(f32[4,192,128]{2,1,0:T(8,128)S(1)} %get-tuple-element.469), channel_id=1, source_target_pairs={{0,4},{4,8},{8,12},{12,16},{16,20},{20,24},{24,28},{28,32},{32,36}... | collective-permute-start | bytes 1179656 | tf_op jit(solution)/shard_map/while/body/eval_jaxpr/ppermute | solution.py:15
  612.7 11.5 %collective-permute-start.2 = (f32[4,192,128]{2,1,0:T(8,128)S(1)}, f32[4,192,128]{2,1,0:T(8,128)S(1)}, u32[]{:S(2)}, u32[]{:S(2)}) collective-permute-start(f32[4,192,128]{2,1,0:T(8,128)S(1)} %get-tuple-element.468), channel_id=1, source_target_pairs={{4,0},{8,4},{12,8},{16,12},{20,16},{24,20},{28,24},{32,28},{36,32}... | collective-permute-start | bytes 1179656 | tf_op jit(solution)/shard_map/while/body/eval_jaxpr/ppermute | solution.py:18
  635.9 19.3 %collective-permute-start.3 = (f32[4,192,128]{2,1,0:T(8,128)S(1)}, f32[4,192,128]{2,1,0:T(8,128)S(1)}, u32[]{:S(2)}, u32[]{:S(2)}) collective-permute-start(f32[4,192,128]{2,1,0:T(8,128)S(1)} %get-tuple-element.469), channel_id=1, source_target_pairs={{0,4},{4,8},{8,12},{12,16},{16,20},{20,24},{24,28},{28,32},{32,36}... | collective-permute-start | bytes 1179656 | tf_op jit(solution)/shard_map/while/body/eval_jaxpr/ppermute | solution.py:15
  640.6 20.2 %collective-permute-start.2 = (f32[4,192,128]{2,1,0:T(8,128)S(1)}, f32[4,192,128]{2,1,0:T(8,128)S(1)}, u32[]{:S(2)}, u32[]{:S(2)}) collective-permute-start(f32[4,192,128]{2,1,0:T(8,128)S(1)} %get-tuple-element.468), channel_id=1, source_target_pairs={{4,0},{8,4},{12,8},{16,12},{20,16},{24,20},{28,24},{32,28},{36,32}... | collective-permute-start | bytes 1179656 | tf_op jit(solution)/shard_map/while/body/eval_jaxpr/ppermute | solution.py:18
  655.4 6.4 copy-start.3
  (34 other events, 93.8 us)
Sparse Core Ops, SparseCore 0:
  672.6 91.8 all-reduce.3
where the time goes:
time: 777 us; the launch traced here: 773 us
  waiting for transfers between devices  349 us (45%)
  other arithmetic  199 us (26%)
  starting transfers between devices  110 us (14%)
  local copies, waits for them, and re-layouts  97.8 us (13%)
  between operations  14.1 us (2%)
    ppermute x20, waiting for transfers between devices, with_halo(): lax.ppermute(lax.slice_in_dim(block, 0, width, axis=dim), axis, backward)  164 us
    ppermute x20, waiting for transfers between devices, with_halo(): lax.ppermute(lax.slice_in_dim(block, block.shape[dim] - width, None, axis...  93.7 us
    psum x1, waiting for transfers between devices, per_device(): summed = lax.psum(imaging, 'shot')  92 us
    ppermute x20, starting transfers between devices, with_halo(): lax.ppermute(lax.slice_in_dim(block, block.shape[dim] - width, None, axis...  84.2 us
    scatter-add x10, other arithmetic, backward(): earlier.reshape(-1).at[receiver_cells].add(residual).reshape(velocity.shape)  37.4 us
    add x10, other arithmetic, backward(): 2.0 * following - furthest + courant_sq * laplace(edge_layers(following))  32.8 us
    add x10, other arithmetic, forward(): latest = 2.0 * current - former + courant_sq * laplace(edge_layers(current))  32.8 us
    while x180, local copies, waits for them, and re-layouts  32.6 us
  transfers between devices with their start and end apart: 41, of which 41 were waited for; matrix products, arithmetic and copies ran while one was open for 4% of the time, Pallas kernels for 0%

commit v1 on v0

--- a/solution.py
+++ b/solution.py
@@ -108,7 +108,8 @@
     band_rows = extent_y // lax.axis_size("shot")
     offset = lax.axis_index("shot") * band_rows
     factor = lax.dynamic_slice_in_dim(-2.0 / velocity**3, offset, band_rows, 1)
-    summed = lax.psum(imaging, "shot")
+    pieces = lax.all_gather(imaging, "shot")
+    summed = jnp.sum(pieces, axis=0)
     own_band = lax.dynamic_slice_in_dim(summed, offset, band_rows, 1)
     return factor * own_band
 

time: 777 us -> 760 us (0.978)
  waiting for transfers between devices: 349 us -> 330 us
    psum x1 -> x0, waiting for transfers between devices: 92 us -> none  [per_device(): summed = lax.psum(imaging, 'shot')]
    all_gather x0 -> x1, waiting for transfers between devices: none -> 73 us  [per_device(): pieces = lax.all_gather(imaging, 'shot')]
where the time goes in v1:
time: 760 us; the launch traced here: 756 us
  waiting for transfers between devices  330 us (43%)
  other arithmetic  202 us (27%)
  starting transfers between devices  110 us (14%)
  local copies, waits for them, and re-layouts  97.8 us (13%)
  between operations  14.1 us (2%)
    ppermute x20, waiting for transfers between devices, with_halo(): lax.ppermute(lax.slice_in_dim(block, 0, width, axis=dim), axis, backward)  164 us
    ppermute x20, waiting for transfers between devices, with_halo(): lax.ppermute(lax.slice_in_dim(block, block.shape[dim] - width, None, axis...  93.7 us
    ppermute x20, starting transfers between devices, with_halo(): lax.ppermute(lax.slice_in_dim(block, block.shape[dim] - width, None, axis...  84.2 us
    all_gather x1, waiting for transfers between devices, per_device(): pieces = lax.all_gather(imaging, 'shot')  73 us
    scatter-add x10, other arithmetic, backward(): earlier.reshape(-1).at[receiver_cells].add(residual).reshape(velocity.shape)  37.4 us
    add x10, other arithmetic, backward(): 2.0 * following - furthest + courant_sq * laplace(edge_layers(following))  32.8 us
    add x10, other arithmetic, forward(): latest = 2.0 * current - former + courant_sq * laplace(edge_layers(current))  32.8 us
    while x180, local copies, waits for them, and re-layouts  32.6 us
  transfers between devices with their start and end apart: 41, of which 41 were waited for; matrix products, arithmetic and copies ran while one was open for 4% of the time, Pallas kernels for 0%

profile of v1, /device:TPU:1, one launch (start us, length us, event | category | flops | bytes accessed | tf_op | source)
XLA Modules:
  0.0 756.1 jit_solution(16264275625847629511)
XLA Ops:
  12.2 333.3 %while.37 = (s32[]{:T(128)}, f32[8,192,128]{2,1,0:T(8,128)S(1)}, f32[8,192,128]{2,1,0:T(8,128)}, f32[10,8,192,128]{3,2,1,0:T(8,128)}, f32[10,512]{1,0:T(8,128)},...) while((s32[]{:T(128)}, f32[8,192,128]{2,1,0:T(8,128)S(1)}, ...), condition=%wide.region_2.3_spmd, body=%wide.region_0.2_spmd.sunk | while | flops 13609986 | bytes 43449096 | solution.py:88
  13.0 4.0 collective-permute-start.1
  22.2 13.2 %collective-permute-done = f32[4,192,128]{2,1,0:T(8,128)S(1)} collective-permute-done((f32[4,192,128]{2,1,0:T(8,128)S(1)}, f32[4,192,128]{2,1,0:T(8,128)S(1)}, u32[]{:S(2)}, u32[]{:S(2)}) %collective-permute-start) | collective-permute-done | bytes 393248 | tf_op jit(solution)/shard_map/while/body/eval_jaxpr/ppermute | solution.py:18
  36.4 3.3 fusion.41
  56.1 4.0 collective-permute-done.1
  60.3 10.1 %collective-permute-done = f32[4,192,128]{2,1,0:T(8,128)S(1)} collective-permute-done((f32[4,192,128]{2,1,0:T(8,128)S(1)}, f32[4,192,128]{2,1,0:T(8,128)S(1)}, u32[]{:S(2)}, u32[]{:S(2)}) %collective-permute-start) | collective-permute-done | bytes 393248 | tf_op jit(solution)/shard_map/while/body/eval_jaxpr/ppermute | solution.py:18
  71.4 3.3 fusion.41
  94.5 9.8 %collective-permute-done = f32[4,192,128]{2,1,0:T(8,128)S(1)} collective-permute-done((f32[4,192,128]{2,1,0:T(8,128)S(1)}, f32[4,192,128]{2,1,0:T(8,128)S(1)}, u32[]{:S(2)}, u32[]{:S(2)}) %collective-permute-start) | collective-permute-done | bytes 393248 | tf_op jit(solution)/shard_map/while/body/eval_jaxpr/ppermute | solution.py:18
  105.3 3.3 fusion.41
  127.4 9.7 %collective-permute-done = f32[4,192,128]{2,1,0:T(8,128)S(1)} collective-permute-done((f32[4,192,128]{2,1,0:T(8,128)S(1)}, f32[4,192,128]{2,1,0:T(8,128)S(1)}, u32[]{:S(2)}, u32[]{:S(2)}) %collective-permute-start) | collective-permute-done | bytes 393248 | tf_op jit(solution)/shard_map/while/body/eval_jaxpr/ppermute | solution.py:18
  138.1 3.3 fusion.41
  159.2 8.4 %collective-permute-done = f32[4,192,128]{2,1,0:T(8,128)S(1)} collective-permute-done((f32[4,192,128]{2,1,0:T(8,128)S(1)}, f32[4,192,128]{2,1,0:T(8,128)S(1)}, u32[]{:S(2)}, u32[]{:S(2)}) %collective-permute-start) | collective-permute-done | bytes 393248 | tf_op jit(solution)/shard_map/while/body/eval_jaxpr/ppermute | solution.py:18
  190.1 8.0 %collective-permute-done = f32[4,192,128]{2,1,0:T(8,128)S(1)} collective-permute-done((f32[4,192,128]{2,1,0:T(8,128)S(1)}, f32[4,192,128]{2,1,0:T(8,128)S(1)}, u32[]{:S(2)}, u32[]{:S(2)}) %collective-permute-start) | collective-permute-done | bytes 393248 | tf_op jit(solution)/shard_map/while/body/eval_jaxpr/ppermute | solution.py:18
  219.2 5.9 collective-permute-done
  245.8 4.1 collective-permute-done.1
  250.1 10.8 %collective-permute-done = f32[4,192,128]{2,1,0:T(8,128)S(1)} collective-permute-done((f32[4,192,128]{2,1,0:T(8,128)S(1)}, f32[4,192,128]{2,1,0:T(8,128)S(1)}, u32[]{:S(2)}, u32[]{:S(2)}) %collective-permute-start) | collective-permute-done | bytes 393248 | tf_op jit(solution)/shard_map/while/body/eval_jaxpr/ppermute | solution.py:18
  261.8 3.3 fusion.41
  275.3 5.2 collective-permute-start.1
  285.8 11.1 %collective-permute-done = f32[4,192,128]{2,1,0:T(8,128)S(1)} collective-permute-done((f32[4,192,128]{2,1,0:T(8,128)S(1)}, f32[4,192,128]{2,1,0:T(8,128)S(1)}, u32[]{:S(2)}, u32[]{:S(2)}) %collective-permute-start) | collective-permute-done | bytes 393248 | tf_op jit(solution)/shard_map/while/body/eval_jaxpr/ppermute | solution.py:18
  311.3 5.2 collective-permute-start.1
  321.8 10.1 %collective-permute-done = f32[4,192,128]{2,1,0:T(8,128)S(1)} collective-permute-done((f32[4,192,128]{2,1,0:T(8,128)S(1)}, f32[4,192,128]{2,1,0:T(8,128)S(1)}, u32[]{:S(2)}, u32[]{:S(2)}) %collective-permute-start) | collective-permute-done | bytes 393248 | tf_op jit(solution)/shard_map/while/body/eval_jaxpr/ppermute | solution.py:18
  346.9 325.5 %while.38 = (s32[]{:T(128)}, f32[8,192,128]{2,1,0:T(8,128)S(1)}, f32[8,192,128]{2,1,0:T(8,128)}, f32[8,192,128]{2,1,0:T(8,128)}, f32[8,192,128]{2,1,0:T(8,128)S(...) while((s32[]{:T(128)}, f32[8,192,128]{2,1,0:T(8,128)S(1)}, ...), condition=%wide.region_5.6_spmd.clone, body=%wide.region_3.5_spmd.clone.sunk | while | flops 13607940 | bytes 49729836 | solution.py:102
  347.0 4.9 collective-permute-start.3
  357.0 6.4 collective-permute-done.2
  368.6 3.7 scatter_fusion.1
  375.0 5.3 collective-permute-start.3
  382.4 12.6 %collective-permute-done.3 = f32[4,192,128]{2,1,0:T(8,128)S(1)} collective-permute-done((f32[4,192,128]{2,1,0:T(8,128)S(1)}, f32[4,192,128]{2,1,0:T(8,128)S(1)}, u32[]{:S(2)}, u32[]{:S(2)}) %collective-permute-start.3) | collective-permute-done | bytes 393248 | tf_op jit(solution)/shard_map/while/body/eval_jaxpr/ppermute | solution.py:15
  395.2 5.2 collective-permute-done.2
  401.3 3.3 fusion.44
  405.6 3.7 scatter_fusion.1
  412.1 5.3 collective-permute-start.3
  419.4 3.3 collective-permute-done.3
  422.9 10.5 %collective-permute-done.2 = f32[4,192,128]{2,1,0:T(8,128)S(1)} collective-permute-done((f32[4,192,128]{2,1,0:T(8,128)S(1)}, f32[4,192,128]{2,1,0:T(8,128)S(1)}, u32[]{:S(2)}, u32[]{:S(2)}) %collective-permute-start.2) | collective-permute-done | bytes 393248 | tf_op jit(solution)/shard_map/while/body/eval_jaxpr/ppermute | solution.py:18
  434.3 3.3 fusion.44
  438.6 3.7 scatter_fusion.1
  445.0 5.2 collective-permute-start.3
  452.3 5.2 collective-permute-done.3
  457.7 7.9 %collective-permute-done.2 = f32[4,192,128]{2,1,0:T(8,128)S(1)} collective-permute-done((f32[4,192,128]{2,1,0:T(8,128)S(1)}, f32[4,192,128]{2,1,0:T(8,128)S(1)}, u32[]{:S(2)}, u32[]{:S(2)}) %collective-permute-start.2) | collective-permute-done | bytes 393248 | tf_op jit(solution)/shard_map/while/body/eval_jaxpr/ppermute | solution.py:18
  470.8 3.7 scatter_fusion.1
  477.3 5.3 collective-permute-start.3
  484.7 5.9 collective-permute-done.3
  490.7 3.4 collective-permute-done.2
  499.3 3.7 scatter_fusion.1
  505.8 4.7 collective-permute-start.3
  512.5 12.5 %collective-permute-done.3 = f32[4,192,128]{2,1,0:T(8,128)S(1)} collective-permute-done((f32[4,192,128]{2,1,0:T(8,128)S(1)}, f32[4,192,128]{2,1,0:T(8,128)S(1)}, u32[]{:S(2)}, u32[]{:S(2)}) %collective-permute-start.3) | collective-permute-done | bytes 393248 | tf_op jit(solution)/shard_map/while/body/eval_jaxpr/ppermute | solution.py:15
  525.3 5.4 collective-permute-done.2
  535.9 3.7 scatter_fusion.1
  542.4 5.0 collective-permute-start.3
  549.4 3.4 collective-permute-done.3
  553.0 10.7 %collective-permute-done.2 = f32[4,192,128]{2,1,0:T(8,128)S(1)} collective-permute-done((f32[4,192,128]{2,1,0:T(8,128)S(1)}, f32[4,192,128]{2,1,0:T(8,128)S(1)}, u32[]{:S(2)}, u32[]{:S(2)}) %collective-permute-start.2) | collective-permute-done | bytes 393248 | tf_op jit(solution)/shard_map/while/body/eval_jaxpr/ppermute | solution.py:18
  568.9 3.7 scatter_fusion.1
  575.4 5.0 collective-permute-start.3
  582.4 5.3 collective-permute-done.3
  587.8 7.9 %collective-permute-done.2 = f32[4,192,128]{2,1,0:T(8,128)S(1)} collective-permute-done((f32[4,192,128]{2,1,0:T(8,128)S(1)}, f32[4,192,128]{2,1,0:T(8,128)S(1)}, u32[]{:S(2)}, u32[]{:S(2)}) %collective-permute-start.2) | collective-permute-done | bytes 393248 | tf_op jit(solution)/shard_map/while/body/eval_jaxpr/ppermute | solution.py:18
  601.0 3.7 scatter_fusion.1
  607.4 5.3 collective-permute-start.3
  614.8 5.9 collective-permute-done.3
  620.8 3.4 collective-permute-done.2
  629.5 3.7 scatter_fusion.1
  635.9 4.7 collective-permute-start.3
  642.6 12.6 %collective-permute-done.3 = f32[4,192,128]{2,1,0:T(8,128)S(1)} collective-permute-done((f32[4,192,128]{2,1,0:T(8,128)S(1)}, f32[4,192,128]{2,1,0:T(8,128)S(1)}, u32[]{:S(2)}, u32[]{:S(2)}) %collective-permute-start.3) | collective-permute-done | bytes 393248 | tf_op jit(solution)/shard_map/while/body/eval_jaxpr/ppermute | solution.py:15
  655.4 5.4 collective-permute-done.2
  666.0 3.7 scatter_fusion.1
  672.5 73.0 %all-gather.3.cloned.1.call-done = f32[32,192,128]{2,1,0:T(8,128)} async-done(((f32[8,192,128]{2,1,0:T(8,128)}), f32[32,192,128]{2,1,0:T(8,128)}) %all-gather.3.cloned.1.call-update) | async-done | bytes 3145744 | tf_op jit(solution)/shard_map/all_gather | solution.py:111
  (427 shorter events, 303.0 us)
Async XLA Ops:
  6.5 738.9 %all-gather.3.cloned.1.call-start = ((), (), s32[]{:S(2)}) async-start(), calls=%async_computation | async-start | bytes 3932160 | tf_op jit(solution)/shard_map/all_gather | solution.py:111
  6.5 5.1 copy-start.11
  6.5 5.7 copy-start
  6.6 5.7 copy-start.8
  12.2 334.7 %copy-start.1 = (f32[1,8,192,128]{3,2,1,0:T(8,128)S(1)}, f32[1,8,192,128]{3,2,1,0:T(8,128)}, u32[]{:S(2)}) copy-start(f32[1,8,192,128]{3,2,1,0:T(8,128)} %param.17) | copy-start | bytes 2359300
  13.0 9.0 %collective-permute-start.1 = (f32[4,192,128]{2,1,0:T(8,128)}, f32[4,192,128]{2,1,0:T(8,128)S(1)}, u32[]{:S(2)}, u32[]{:S(2)}) collective-permute-start(f32[4,192,128]{2,1,0:T(8,128)} %get-tuple-element.457), channel_id=1, source_target_pairs={{0,4},{4,8},{8,12},{12,16},{16,20},{20,24},{24,28},{28,32},{32,36}... | collective-permute-start | bytes 1179656 | tf_op jit(solution)/shard_map/while/body/eval_jaxpr/ppermute | solution.py:15
  17.0 18.4 %collective-permute-start = (f32[4,192,128]{2,1,0:T(8,128)S(1)}, f32[4,192,128]{2,1,0:T(8,128)S(1)}, u32[]{:S(2)}, u32[]{:S(2)}) collective-permute-start(f32[4,192,128]{2,1,0:T(8,128)S(1)} %get-tuple-element.456), channel_id=1, source_target_pairs={{4,0},{8,4},{12,8},{16,12},{20,16},{24,20},{28,24},{32,28},{36,32}... | collective-permute-start | bytes 1179656 | tf_op jit(solution)/shard_map/while/body/eval_jaxpr/ppermute | solution.py:18
  22.2 14.2 %copy-start.2 = (f32[8,192,128]{2,1,0:T(8,128)S(1)}, f32[8,192,128]{2,1,0:T(8,128)}, u32[]{:S(2)}) copy-start(f32[8,192,128]{2,1,0:T(8,128)} %get-tuple-element.485) | copy-start | bytes 2359300 | tf_op jit(solution)/shard_map/while
  49.9 10.3 %collective-permute-start.1 = (f32[4,192,128]{2,1,0:T(8,128)}, f32[4,192,128]{2,1,0:T(8,128)S(1)}, u32[]{:S(2)}, u32[]{:S(2)}) collective-permute-start(f32[4,192,128]{2,1,0:T(8,128)} %get-tuple-element.457), channel_id=1, source_target_pairs={{0,4},{4,8},{8,12},{12,16},{16,20},{20,24},{24,28},{28,32},{32,36}... | collective-permute-start | bytes 1179656 | tf_op jit(solution)/shard_map/while/body/eval_jaxpr/ppermute | solution.py:15
  53.0 17.5 %collective-permute-start = (f32[4,192,128]{2,1,0:T(8,128)S(1)}, f32[4,192,128]{2,1,0:T(8,128)S(1)}, u32[]{:S(2)}, u32[]{:S(2)}) collective-permute-start(f32[4,192,128]{2,1,0:T(8,128)S(1)} %get-tuple-element.456), channel_id=1, source_target_pairs={{4,0},{8,4},{12,8},{16,12},{20,16},{24,20},{28,24},{32,28},{36,32}... | collective-permute-start | bytes 1179656 | tf_op jit(solution)/shard_map/while/body/eval_jaxpr/ppermute | solution.py:18
  60.3 11.1 %copy-start.2 = (f32[8,192,128]{2,1,0:T(8,128)S(1)}, f32[8,192,128]{2,1,0:T(8,128)}, u32[]{:S(2)}) copy-start(f32[8,192,128]{2,1,0:T(8,128)} %get-tuple-element.485) | copy-start | bytes 2359300 | tf_op jit(solution)/shard_map/while
  84.9 9.3 %collective-permute-start.1 = (f32[4,192,128]{2,1,0:T(8,128)}, f32[4,192,128]{2,1,0:T(8,128)S(1)}, u32[]{:S(2)}, u32[]{:S(2)}) collective-permute-start(f32[4,192,128]{2,1,0:T(8,128)} %get-tuple-element.457), channel_id=1, source_target_pairs={{0,4},{4,8},{8,12},{12,16},{16,20},{20,24},{24,28},{28,32},{32,36}... | collective-permute-start | bytes 1179656 | tf_op jit(solution)/shard_map/while/body/eval_jaxpr/ppermute | solution.py:15
  88.1 16.2 %collective-permute-start = (f32[4,192,128]{2,1,0:T(8,128)S(1)}, f32[4,192,128]{2,1,0:T(8,128)S(1)}, u32[]{:S(2)}, u32[]{:S(2)}) collective-permute-start(f32[4,192,128]{2,1,0:T(8,128)S(1)} %get-tuple-element.456), channel_id=1, source_target_pairs={{4,0},{8,4},{12,8},{16,12},{20,16},{24,20},{28,24},{32,28},{36,32}... | collective-permute-start | bytes 1179656 | tf_op jit(solution)/shard_map/while/body/eval_jaxpr/ppermute | solution.py:18
  94.5 10.8 %copy-start.2 = (f32[8,192,128]{2,1,0:T(8,128)S(1)}, f32[8,192,128]{2,1,0:T(8,128)}, u32[]{:S(2)}) copy-start(f32[8,192,128]{2,1,0:T(8,128)} %get-tuple-element.485) | copy-start | bytes 2359300 | tf_op jit(solution)/shard_map/while
  118.8 8.4 %collective-permute-start.1 = (f32[4,192,128]{2,1,0:T(8,128)}, f32[4,192,128]{2,1,0:T(8,128)S(1)}, u32[]{:S(2)}, u32[]{:S(2)}) collective-permute-start(f32[4,192,128]{2,1,0:T(8,128)} %get-tuple-element.457), channel_id=1, source_target_pairs={{0,4},{4,8},{8,12},{12,16},{16,20},{20,24},{24,28},{28,32},{32,36}... | collective-permute-start | bytes 1179656 | tf_op jit(solution)/shard_map/while/body/eval_jaxpr/ppermute | solution.py:15
  121.9 15.2 %collective-permute-start = (f32[4,192,128]{2,1,0:T(8,128)S(1)}, f32[4,192,128]{2,1,0:T(8,128)S(1)}, u32[]{:S(2)}, u32[]{:S(2)}) collective-permute-start(f32[4,192,128]{2,1,0:T(8,128)S(1)} %get-tuple-element.456), channel_id=1, source_target_pairs={{4,0},{8,4},{12,8},{16,12},{20,16},{24,20},{28,24},{32,28},{36,32}... | collective-permute-start | bytes 1179656 | tf_op jit(solution)/shard_map/while/body/eval_jaxpr/ppermute | solution.py:18
  127.4 10.7 %copy-start.2 = (f32[8,192,128]{2,1,0:T(8,128)S(1)}, f32[8,192,128]{2,1,0:T(8,128)}, u32[]{:S(2)}) copy-start(f32[8,192,128]{2,1,0:T(8,128)} %get-tuple-element.485) | copy-start | bytes 2359300 | tf_op jit(solution)/shard_map/while
  151.5 7.5 collective-permute-start.1
  154.0 13.6 %collective-permute-start = (f32[4,192,128]{2,1,0:T(8,128)S(1)}, f32[4,192,128]{2,1,0:T(8,128)S(1)}, u32[]{:S(2)}, u32[]{:S(2)}) collective-permute-start(f32[4,192,128]{2,1,0:T(8,128)S(1)} %get-tuple-element.456), channel_id=1, source_target_pairs={{4,0},{8,4},{12,8},{16,12},{20,16},{24,20},{28,24},{32,28},{36,32}... | collective-permute-start | bytes 1179656 | tf_op jit(solution)/shard_map/while/body/eval_jaxpr/ppermute | solution.py:18
  159.2 9.4 %copy-start.2 = (f32[8,192,128]{2,1,0:T(8,128)S(1)}, f32[8,192,128]{2,1,0:T(8,128)}, u32[]{:S(2)}) copy-start(f32[8,192,128]{2,1,0:T(8,128)} %get-tuple-element.485) | copy-start | bytes 2359300 | tf_op jit(solution)/shard_map/while
  182.1 7.8 %collective-permute-start.1 = (f32[4,192,128]{2,1,0:T(8,128)}, f32[4,192,128]{2,1,0:T(8,128)S(1)}, u32[]{:S(2)}, u32[]{:S(2)}) collective-permute-start(f32[4,192,128]{2,1,0:T(8,128)} %get-tuple-element.457), channel_id=1, source_target_pairs={{0,4},{4,8},{8,12},{12,16},{16,20},{20,24},{24,28},{28,32},{32,36}... | collective-permute-start | bytes 1179656 | tf_op jit(solution)/shard_map/while/body/eval_jaxpr/ppermute | solution.py:15
  184.9 13.2 %collective-permute-start = (f32[4,192,128]{2,1,0:T(8,128)S(1)}, f32[4,192,128]{2,1,0:T(8,128)S(1)}, u32[]{:S(2)}, u32[]{:S(2)}) collective-permute-start(f32[4,192,128]{2,1,0:T(8,128)S(1)} %get-tuple-element.456), channel_id=1, source_target_pairs={{4,0},{8,4},{12,8},{16,12},{20,16},{24,20},{28,24},{32,28},{36,32}... | collective-permute-start | bytes 1179656 | tf_op jit(solution)/shard_map/while/body/eval_jaxpr/ppermute | solution.py:18
  190.0 9.0 %copy-start.2 = (f32[8,192,128]{2,1,0:T(8,128)S(1)}, f32[8,192,128]{2,1,0:T(8,128)}, u32[]{:S(2)}) copy-start(f32[8,192,128]{2,1,0:T(8,128)} %get-tuple-element.485) | copy-start | bytes 2359300 | tf_op jit(solution)/shard_map/while
  212.5 6.5 collective-permute-start.1
  214.0 11.1 %collective-permute-start = (f32[4,192,128]{2,1,0:T(8,128)S(1)}, f32[4,192,128]{2,1,0:T(8,128)S(1)}, u32[]{:S(2)}, u32[]{:S(2)}) collective-permute-start(f32[4,192,128]{2,1,0:T(8,128)S(1)} %get-tuple-element.456), channel_id=1, source_target_pairs={{4,0},{8,4},{12,8},{16,12},{20,16},{24,20},{28,24},{32,28},{36,32}... | collective-permute-start | bytes 1179656 | tf_op jit(solution)/shard_map/while/body/eval_jaxpr/ppermute | solution.py:18
  219.2 6.9 copy-start.2
  239.6 10.3 %collective-permute-start.1 = (f32[4,192,128]{2,1,0:T(8,128)}, f32[4,192,128]{2,1,0:T(8,128)S(1)}, u32[]{:S(2)}, u32[]{:S(2)}) collective-permute-start(f32[4,192,128]{2,1,0:T(8,128)} %get-tuple-element.457), channel_id=1, source_target_pairs={{0,4},{4,8},{8,12},{12,16},{16,20},{20,24},{24,28},{28,32},{32,36}... | collective-permute-start | bytes 1179656 | tf_op jit(solution)/shard_map/while/body/eval_jaxpr/ppermute | solution.py:15
  242.6 18.3 %collective-permute-start = (f32[4,192,128]{2,1,0:T(8,128)S(1)}, f32[4,192,128]{2,1,0:T(8,128)S(1)}, u32[]{:S(2)}, u32[]{:S(2)}) collective-permute-start(f32[4,192,128]{2,1,0:T(8,128)S(1)} %get-tuple-element.456), channel_id=1, source_target_pairs={{4,0},{8,4},{12,8},{16,12},{20,16},{24,20},{28,24},{32,28},{36,32}... | collective-permute-start | bytes 1179656 | tf_op jit(solution)/shard_map/while/body/eval_jaxpr/ppermute | solution.py:18
  250.0 11.8 %copy-start.2 = (f32[8,192,128]{2,1,0:T(8,128)S(1)}, f32[8,192,128]{2,1,0:T(8,128)}, u32[]{:S(2)}) copy-start(f32[8,192,128]{2,1,0:T(8,128)} %get-tuple-element.485) | copy-start | bytes 2359300 | tf_op jit(solution)/shard_map/while
  275.3 10.2 %collective-permute-start.1 = (f32[4,192,128]{2,1,0:T(8,128)}, f32[4,192,128]{2,1,0:T(8,128)S(1)}, u32[]{:S(2)}, u32[]{:S(2)}) collective-permute-start(f32[4,192,128]{2,1,0:T(8,128)} %get-tuple-element.457), channel_id=1, source_target_pairs={{0,4},{4,8},{8,12},{12,16},{16,20},{20,24},{24,28},{28,32},{32,36}... | collective-permute-start | bytes 1179656 | tf_op jit(solution)/shard_map/while/body/eval_jaxpr/ppermute | solution.py:15
  280.6 16.3 %collective-permute-start = (f32[4,192,128]{2,1,0:T(8,128)S(1)}, f32[4,192,128]{2,1,0:T(8,128)S(1)}, u32[]{:S(2)}, u32[]{:S(2)}) collective-permute-start(f32[4,192,128]{2,1,0:T(8,128)S(1)} %get-tuple-element.456), channel_id=1, source_target_pairs={{4,0},{8,4},{12,8},{16,12},{20,16},{24,20},{28,24},{32,28},{36,32}... | collective-permute-start | bytes 1179656 | tf_op jit(solution)/shard_map/while/body/eval_jaxpr/ppermute | solution.py:18
  285.8 12.0 %copy-start.2 = (f32[8,192,128]{2,1,0:T(8,128)S(1)}, f32[8,192,128]{2,1,0:T(8,128)}, u32[]{:S(2)}) copy-start(f32[8,192,128]{2,1,0:T(8,128)} %get-tuple-element.485) | copy-start | bytes 2359300 | tf_op jit(solution)/shard_map/while
  311.3 10.2 %collective-permute-start.1 = (f32[4,192,128]{2,1,0:T(8,128)}, f32[4,192,128]{2,1,0:T(8,128)S(1)}, u32[]{:S(2)}, u32[]{:S(2)}) collective-permute-start(f32[4,192,128]{2,1,0:T(8,128)} %get-tuple-element.457), channel_id=1, source_target_pairs={{0,4},{4,8},{8,12},{12,16},{16,20},{20,24},{24,28},{28,32},{32,36}... | collective-permute-start | bytes 1179656 | tf_op jit(solution)/shard_map/while/body/eval_jaxpr/ppermute | solution.py:15
  316.6 15.3 %collective-permute-start = (f32[4,192,128]{2,1,0:T(8,128)S(1)}, f32[4,192,128]{2,1,0:T(8,128)S(1)}, u32[]{:S(2)}, u32[]{:S(2)}) collective-permute-start(f32[4,192,128]{2,1,0:T(8,128)S(1)} %get-tuple-element.456), channel_id=1, source_target_pairs={{4,0},{8,4},{12,8},{16,12},{20,16},{24,20},{28,24},{32,28},{36,32}... | collective-permute-start | bytes 1179656 | tf_op jit(solution)/shard_map/while/body/eval_jaxpr/ppermute | solution.py:18
  321.8 11.1 %copy-start.2 = (f32[8,192,128]{2,1,0:T(8,128)S(1)}, f32[8,192,128]{2,1,0:T(8,128)}, u32[]{:S(2)}) copy-start(f32[8,192,128]{2,1,0:T(8,128)} %get-tuple-element.485) | copy-start | bytes 2359300 | tf_op jit(solution)/shard_map/while
  347.0 9.8 %collective-permute-start.3 = (f32[4,192,128]{2,1,0:T(8,128)S(1)}, f32[4,192,128]{2,1,0:T(8,128)S(1)}, u32[]{:S(2)}, u32[]{:S(2)}) collective-permute-start(f32[4,192,128]{2,1,0:T(8,128)S(1)} %get-tuple-element.469), channel_id=1, source_target_pairs={{0,4},{4,8},{8,12},{12,16},{16,20},{20,24},{24,28},{28,32},{32,36}... | collective-permute-start | bytes 1179656 | tf_op jit(solution)/shard_map/while/body/eval_jaxpr/ppermute | solution.py:15
  351.9 11.4 %collective-permute-start.2 = (f32[4,192,128]{2,1,0:T(8,128)S(1)}, f32[4,192,128]{2,1,0:T(8,128)S(1)}, u32[]{:S(2)}, u32[]{:S(2)}) collective-permute-start(f32[4,192,128]{2,1,0:T(8,128)S(1)} %get-tuple-element.468), channel_id=1, source_target_pairs={{4,0},{8,4},{12,8},{16,12},{20,16},{24,20},{28,24},{32,28},{36,32}... | collective-permute-start | bytes 1179656 | tf_op jit(solution)/shard_map/while/body/eval_jaxpr/ppermute | solution.py:18
  357.0 7.3 copy-start.3
  375.0 20.0 %collective-permute-start.3 = (f32[4,192,128]{2,1,0:T(8,128)S(1)}, f32[4,192,128]{2,1,0:T(8,128)S(1)}, u32[]{:S(2)}, u32[]{:S(2)}) collective-permute-start(f32[4,192,128]{2,1,0:T(8,128)S(1)} %get-tuple-element.469), channel_id=1, source_target_pairs={{0,4},{4,8},{8,12},{12,16},{16,20},{20,24},{24,28},{28,32},{32,36}... | collective-permute-start | bytes 1179656 | tf_op jit(solution)/shard_map/while/body/eval_jaxpr/ppermute | solution.py:15
  380.4 20.0 %collective-permute-start.2 = (f32[4,192,128]{2,1,0:T(8,128)S(1)}, f32[4,192,128]{2,1,0:T(8,128)S(1)}, u32[]{:S(2)}, u32[]{:S(2)}) collective-permute-start(f32[4,192,128]{2,1,0:T(8,128)S(1)} %get-tuple-element.468), channel_id=1, source_target_pairs={{4,0},{8,4},{12,8},{16,12},{20,16},{24,20},{28,24},{32,28},{36,32}... | collective-permute-start | bytes 1179656 | tf_op jit(solution)/shard_map/while/body/eval_jaxpr/ppermute | solution.py:18
  395.2 6.1 copy-start.3
  412.1 10.6 %collective-permute-start.3 = (f32[4,192,128]{2,1,0:T(8,128)S(1)}, f32[4,192,128]{2,1,0:T(8,128)S(1)}, u32[]{:S(2)}, u32[]{:S(2)}) collective-permute-start(f32[4,192,128]{2,1,0:T(8,128)S(1)} %get-tuple-element.469), channel_id=1, source_target_pairs={{0,4},{4,8},{8,12},{12,16},{16,20},{20,24},{24,28},{28,32},{32,36}... | collective-permute-start | bytes 1179656 | tf_op jit(solution)/shard_map/while/body/eval_jaxpr/ppermute | solution.py:15
  417.3 16.0 %collective-permute-start.2 = (f32[4,192,128]{2,1,0:T(8,128)S(1)}, f32[4,192,128]{2,1,0:T(8,128)S(1)}, u32[]{:S(2)}, u32[]{:S(2)}) collective-permute-start(f32[4,192,128]{2,1,0:T(8,128)S(1)} %get-tuple-element.468), channel_id=1, source_target_pairs={{4,0},{8,4},{12,8},{16,12},{20,16},{24,20},{28,24},{32,28},{36,32}... | collective-permute-start | bytes 1179656 | tf_op jit(solution)/shard_map/while/body/eval_jaxpr/ppermute | solution.py:18
  422.9 11.5 %copy-start.3 = (f32[8,192,128]{2,1,0:T(8,128)S(1)}, f32[8,192,128]{2,1,0:T(8,128)}, u32[]{:S(2)}) copy-start(f32[8,192,128]{2,1,0:T(8,128)} %get-tuple-element.518) | copy-start | bytes 2359300 | tf_op jit(solution)/shard_map/while
  445.0 12.5 %collective-permute-start.3 = (f32[4,192,128]{2,1,0:T(8,128)S(1)}, f32[4,192,128]{2,1,0:T(8,128)S(1)}, u32[]{:S(2)}, u32[]{:S(2)}) collective-permute-start(f32[4,192,128]{2,1,0:T(8,128)S(1)} %get-tuple-element.469), channel_id=1, source_target_pairs={{0,4},{4,8},{8,12},{12,16},{16,20},{20,24},{24,28},{28,32},{32,36}... | collective-permute-start | bytes 1179656 | tf_op jit(solution)/shard_map/while/body/eval_jaxpr/ppermute | solution.py:15
  450.3 15.4 %collective-permute-start.2 = (f32[4,192,128]{2,1,0:T(8,128)S(1)}, f32[4,192,128]{2,1,0:T(8,128)S(1)}, u32[]{:S(2)}, u32[]{:S(2)}) collective-permute-start(f32[4,192,128]{2,1,0:T(8,128)S(1)} %get-tuple-element.468), channel_id=1, source_target_pairs={{4,0},{8,4},{12,8},{16,12},{20,16},{24,20},{28,24},{32,28},{36,32}... | collective-permute-start | bytes 1179656 | tf_op jit(solution)/shard_map/while/body/eval_jaxpr/ppermute | solution.py:18
  457.7 8.9 %copy-start.3 = (f32[8,192,128]{2,1,0:T(8,128)S(1)}, f32[8,192,128]{2,1,0:T(8,128)}, u32[]{:S(2)}) copy-start(f32[8,192,128]{2,1,0:T(8,128)} %get-tuple-element.518) | copy-start | bytes 2359300 | tf_op jit(solution)/shard_map/while
  477.3 13.2 %collective-permute-start.3 = (f32[4,192,128]{2,1,0:T(8,128)S(1)}, f32[4,192,128]{2,1,0:T(8,128)S(1)}, u32[]{:S(2)}, u32[]{:S(2)}) collective-permute-start(f32[4,192,128]{2,1,0:T(8,128)S(1)} %get-tuple-element.469), channel_id=1, source_target_pairs={{0,4},{4,8},{8,12},{12,16},{16,20},{20,24},{24,28},{28,32},{32,36}... | collective-permute-start | bytes 1179656 | tf_op jit(solution)/shard_map/while/body/eval_jaxpr/ppermute | solution.py:15
  482.6 11.5 %collective-permute-start.2 = (f32[4,192,128]{2,1,0:T(8,128)S(1)}, f32[4,192,128]{2,1,0:T(8,128)S(1)}, u32[]{:S(2)}, u32[]{:S(2)}) collective-permute-start(f32[4,192,128]{2,1,0:T(8,128)S(1)} %get-tuple-element.468), channel_id=1, source_target_pairs={{4,0},{8,4},{12,8},{16,12},{20,16},{24,20},{28,24},{32,28},{36,32}... | collective-permute-start | bytes 1179656 | tf_op jit(solution)/shard_map/while/body/eval_jaxpr/ppermute | solution.py:18
  490.7 4.4 copy-start.3
  505.8 19.3 %collective-permute-start.3 = (f32[4,192,128]{2,1,0:T(8,128)S(1)}, f32[4,192,128]{2,1,0:T(8,128)S(1)}, u32[]{:S(2)}, u32[]{:S(2)}) collective-permute-start(f32[4,192,128]{2,1,0:T(8,128)S(1)} %get-tuple-element.469), channel_id=1, source_target_pairs={{0,4},{4,8},{8,12},{12,16},{16,20},{20,24},{24,28},{28,32},{32,36}... | collective-permute-start | bytes 1179656 | tf_op jit(solution)/shard_map/while/body/eval_jaxpr/ppermute | solution.py:15
  510.5 20.2 %collective-permute-start.2 = (f32[4,192,128]{2,1,0:T(8,128)S(1)}, f32[4,192,128]{2,1,0:T(8,128)S(1)}, u32[]{:S(2)}, u32[]{:S(2)}) collective-permute-start(f32[4,192,128]{2,1,0:T(8,128)S(1)} %get-tuple-element.468), channel_id=1, source_target_pairs={{4,0},{8,4},{12,8},{16,12},{20,16},{24,20},{28,24},{32,28},{36,32}... | collective-permute-start | bytes 1179656 | tf_op jit(solution)/shard_map/while/body/eval_jaxpr/ppermute | solution.py:18
  525.3 6.4 copy-start.3
  542.4 10.4 %collective-permute-start.3 = (f32[4,192,128]{2,1,0:T(8,128)S(1)}, f32[4,192,128]{2,1,0:T(8,128)S(1)}, u32[]{:S(2)}, u32[]{:S(2)}) collective-permute-start(f32[4,192,128]{2,1,0:T(8,128)S(1)} %get-tuple-element.469), channel_id=1, source_target_pairs={{0,4},{4,8},{8,12},{12,16},{16,20},{20,24},{24,28},{28,32},{32,36}... | collective-permute-start | bytes 1179656 | tf_op jit(solution)/shard_map/while/body/eval_jaxpr/ppermute | solution.py:15
  547.3 16.4 %collective-permute-start.2 = (f32[4,192,128]{2,1,0:T(8,128)S(1)}, f32[4,192,128]{2,1,0:T(8,128)S(1)}, u32[]{:S(2)}, u32[]{:S(2)}) collective-permute-start(f32[4,192,128]{2,1,0:T(8,128)S(1)} %get-tuple-element.468), channel_id=1, source_target_pairs={{4,0},{8,4},{12,8},{16,12},{20,16},{24,20},{28,24},{32,28},{36,32}... | collective-permute-start | bytes 1179656 | tf_op jit(solution)/shard_map/while/body/eval_jaxpr/ppermute | solution.py:18
  553.0 11.7 %copy-start.3 = (f32[8,192,128]{2,1,0:T(8,128)S(1)}, f32[8,192,128]{2,1,0:T(8,128)}, u32[]{:S(2)}) copy-start(f32[8,192,128]{2,1,0:T(8,128)} %get-tuple-element.518) | copy-start | bytes 2359300 | tf_op jit(solution)/shard_map/while
  575.4 12.3 %collective-permute-start.3 = (f32[4,192,128]{2,1,0:T(8,128)S(1)}, f32[4,192,128]{2,1,0:T(8,128)S(1)}, u32[]{:S(2)}, u32[]{:S(2)}) collective-permute-start(f32[4,192,128]{2,1,0:T(8,128)S(1)} %get-tuple-element.469), channel_id=1, source_target_pairs={{0,4},{4,8},{8,12},{12,16},{16,20},{20,24},{24,28},{28,32},{32,36}... | collective-permute-start | bytes 1179656 | tf_op jit(solution)/shard_map/while/body/eval_jaxpr/ppermute | solution.py:15
  580.3 15.4 %collective-permute-start.2 = (f32[4,192,128]{2,1,0:T(8,128)S(1)}, f32[4,192,128]{2,1,0:T(8,128)S(1)}, u32[]{:S(2)}, u32[]{:S(2)}) collective-permute-start(f32[4,192,128]{2,1,0:T(8,128)S(1)} %get-tuple-element.468), channel_id=1, source_target_pairs={{4,0},{8,4},{12,8},{16,12},{20,16},{24,20},{28,24},{32,28},{36,32}... | collective-permute-start | bytes 1179656 | tf_op jit(solution)/shard_map/while/body/eval_jaxpr/ppermute | solution.py:18
  587.8 8.9 %copy-start.3 = (f32[8,192,128]{2,1,0:T(8,128)S(1)}, f32[8,192,128]{2,1,0:T(8,128)}, u32[]{:S(2)}) copy-start(f32[8,192,128]{2,1,0:T(8,128)} %get-tuple-element.518) | copy-start | bytes 2359300 | tf_op jit(solution)/shard_map/while
  607.4 13.2 %collective-permute-start.3 = (f32[4,192,128]{2,1,0:T(8,128)S(1)}, f32[4,192,128]{2,1,0:T(8,128)S(1)}, u32[]{:S(2)}, u32[]{:S(2)}) collective-permute-start(f32[4,192,128]{2,1,0:T(8,128)S(1)} %get-tuple-element.469), channel_id=1, source_target_pairs={{0,4},{4,8},{8,12},{12,16},{16,20},{20,24},{24,28},{28,32},{32,36}... | collective-permute-start | bytes 1179656 | tf_op jit(solution)/shard_map/while/body/eval_jaxpr/ppermute | solution.py:15
  612.7 11.5 %collective-permute-start.2 = (f32[4,192,128]{2,1,0:T(8,128)S(1)}, f32[4,192,128]{2,1,0:T(8,128)S(1)}, u32[]{:S(2)}, u32[]{:S(2)}) collective-permute-start(f32[4,192,128]{2,1,0:T(8,128)S(1)} %get-tuple-element.468), channel_id=1, source_target_pairs={{4,0},{8,4},{12,8},{16,12},{20,16},{24,20},{28,24},{32,28},{36,32}... | collective-permute-start | bytes 1179656 | tf_op jit(solution)/shard_map/while/body/eval_jaxpr/ppermute | solution.py:18
  635.9 19.3 %collective-permute-start.3 = (f32[4,192,128]{2,1,0:T(8,128)S(1)}, f32[4,192,128]{2,1,0:T(8,128)S(1)}, u32[]{:S(2)}, u32[]{:S(2)}) collective-permute-start(f32[4,192,128]{2,1,0:T(8,128)S(1)} %get-tuple-element.469), channel_id=1, source_target_pairs={{0,4},{4,8},{8,12},{12,16},{16,20},{20,24},{24,28},{28,32},{32,36}... | collective-permute-start | bytes 1179656 | tf_op jit(solution)/shard_map/while/body/eval_jaxpr/ppermute | solution.py:15
  640.6 20.2 %collective-permute-start.2 = (f32[4,192,128]{2,1,0:T(8,128)S(1)}, f32[4,192,128]{2,1,0:T(8,128)S(1)}, u32[]{:S(2)}, u32[]{:S(2)}) collective-permute-start(f32[4,192,128]{2,1,0:T(8,128)S(1)} %get-tuple-element.468), channel_id=1, source_target_pairs={{4,0},{8,4},{12,8},{16,12},{20,16},{24,20},{28,24},{32,28},{36,32}... | collective-permute-start | bytes 1179656 | tf_op jit(solution)/shard_map/while/body/eval_jaxpr/ppermute | solution.py:18
  655.4 6.4 copy-start.3
  (34 other events, 93.8 us)
Sparse Core Ops, SparseCore 0:
  672.6 72.8 all-gather.2
